TPU v7x, 256 devices: a whole 4x4x8 slice. The times are simulated.
256 devices in a mesh: task: 8 (over z_hi, core), row: 8 (over x, z_lo), col: 4 (over y).
Axes of the slice: x: 4, y: 4, z: 8 (z_hi: 4, z_lo: 2; z = z_hi * 2 + z_lo), core: 2. Of those that a mesh axis runs over, the one named last changes fastest.
Arguments:
- activations: bfloat16 [8, 512, 13824], P('task', 'col', 'row'), may hold values from -6 to 6
- weights: bfloat16 [8, 13824, 5120], P('task', 'row', 'col'), may hold values from -0.0625 to 0.0625
- labels: int32 [8, 512], P('task'), may hold values from 0 to 127
- prototypes: bfloat16 [8, 128, 5120], P('task', None, 'col'), may hold values from -6 to 6
Outputs:
- merged: bfloat16 [13824, 5120], P('row', 'col')
- merged_out: bfloat16 [8, 512, 5120], P('task', 'row', 'col')
All inputs are finite; a program needn't handle non-finite values.
Results may differ from a plain program's by a relative error of at most 0.02.
Values may be sent and summed in bfloat16 or wider, within the bound.
A program may use at most 128 MiB of HBM per device.

v0:
```python
import jax
import jax.numpy as jnp
from jax import lax
from jax.sharding import PartitionSpec as P


def class_targets(label_rows, protos):
    count = label_rows.shape[0]
    onehot = (
        label_rows[:, None] == lax.broadcasted_iota(jnp.int32, (count, protos.shape[0]), 1)
    ).astype(jnp.bfloat16)
    return jnp.dot(onehot, protos, preferred_element_type=jnp.float32)


def local(activations, weights, labels, prototypes):
    acts = activations[0]
    weight = weights[0]
    label_row = labels[0]
    protos = prototypes[0]
    full_acts = lax.all_gather(acts, "col", axis=0, tiled=True)
    partial_out = jnp.dot(full_acts, weight, preferred_element_type=jnp.float32)
    output = lax.psum(partial_out.astype(jnp.bfloat16), "row").astype(jnp.float32)
    grad = output - class_targets(label_row, protos)
    gsq = (grad * grad).astype(jnp.bfloat16)
    wide = full_acts.astype(jnp.float32)
    asq = (wide * wide).astype(jnp.bfloat16)
    fisher = lax.dot_general(asq, gsq, (((0,), (0,)), ((), ())), preferred_element_type=jnp.float32)
    weighted = fisher * weight.astype(jnp.float32)
    numer, denom = (
        lax.psum_scatter(weighted, "task", scatter_dimension=0, tiled=True),
        lax.psum_scatter(fisher, "task", scatter_dimension=0, tiled=True),
    )
    piece = (numer / (denom + 1e-06)).astype(jnp.bfloat16)
    merged = lax.all_gather(piece, "task", axis=0, tiled=True)
    result = lax.psum_scatter(
        jnp.dot(full_acts, merged, preferred_element_type=jnp.float32).astype(jnp.bfloat16),
        "row",
        scatter_dimension=0,
        tiled=True,
    )
    return (merged, result[None])


def solution(mesh):
    placed = (
        P("task", "col", "row"),
        P("task", "row", "col"),
        P("task", None),
        P("task", None, "col"),
    )
    return jax.shard_map(
        local,
        mesh=mesh,
        in_specs=placed,
        out_specs=(P("row", "col"), P("task", "row", "col")),
        check_vma=False,
    )
```

profile of v0, /device:TPU:8, one launch (start us, length us, event | category | flops | bytes accessed | tf_op | source)
XLA Modules:
  0.0 475.8 jit_solution(1805810077636972893)
XLA Ops:
  7.2 0.0 copy-start
  7.2 0.0 all-gather.6.cloned.1.call-start
  7.2 0.7 all-gather.6.cloned.1.call-update
  7.9 0.0 copy-start.2
  7.9 0.0 all-reduce.2.cloned.1.call-start
  8.0 38.4 %all-gather.6.cloned.1.call-done = bf16[1,512,1728]{1,2,0:T(8,128)(2,1)} async-done(((bf16[1,128,1728]{1,2,0:T(8,128)(2,1)}), bf16[1,512,1728]{1,2,0:T(8,128)(2,1)}) %all-gather.6.cloned.1.call-update) | async-done | bytes 1769488 | tf_op jit(solution)/shard_map/all_gather | solution.py:20
  46.4 0.0 copy-start.1
  46.4 6.6 %fusion.4 = bf16[512,1280]{1,0:T(8,128)(2,1)} fusion(bf16[1,1728,1280]{2,1,0:T(8,128)(2,1)} %param.5, bf16[1,512,1728]{1,2,0:T(8,128)(2,1)} %all-gather.6.cloned.1.call-done), kind=kOutput, calls=%fused_computation.7 | convolution fusion | flops 2265579520 | bytes 7503872 | tf_op jit(solution)/shard_map/dot_general | solution.py:21
  53.0 0.0 all-reduce.2.cloned.1.call-update
  53.0 0.0 reduce-scatter.6.cloned.1.call-start
  53.1 90.5 %all-reduce.2.cloned.1.call-done = bf16[512,1280]{1,0:T(8,128)(2,1)} async-done(((bf16[512,1280]{1,0:T(8,128)(2,1)}), bf16[512,1280]{1,0:T(8,128)(2,1)}) %all-reduce.2.cloned.1.call-update) | async-done | bytes 1310736 | tf_op jit(solution)/shard_map/psum | solution.py:22
  143.6 0.0 copy-done
  143.6 0.0 copy-done.2
  143.6 0.0 copy-done.1
  143.6 9.8 %convert_multiply_fusion = (f32[1728,1280]{1,0:T(8,128)}, f32[1728,1280]{1,0:T(8,128)}) fusion(bf16[1,1728,1280]{2,1,0:T(8,128)(2,1)} %param.5, bf16[512,1280]{1,0:T(8,128)(2,1)} %all-reduce.2.cloned.1.call-done, bf16[1,128,1280]{2,1,0:T(8,128)(2,1)S(1)} %copy-done, s32[512]{0:T(512)S(1)} %bitcast.30, bf16[1,512,1728]{1,2,0:T(8,128)(2,1)S(1)} %copy-done.1), kind=kOutput, calls=%fused_computation | convolution fusion | flops 2442461184 | bytes 25528320 | tf_op jit(solution)/shard_map/dot_general | solution.py:27
  153.4 0.0 reduce-scatter.6.cloned.1.call-update
  153.4 0.0 reduce-scatter.8.cloned.1.call-start
  153.4 0.5 reduce-scatter.8.cloned.1.call-update
  154.0 0.0 all-gather.4.cloned.1.call-start
  154.0 96.8 %reduce-scatter.6.cloned.1.call-done = f32[216,1280]{1,0:T(8,128)} async-done(((f32[1728,1280]{1,0:T(8,128)}), f32[216,1280]{1,0:T(8,128)}) %reduce-scatter.6.cloned.1.call-update) | async-done | bytes 1105936 | tf_op jit(solution)/shard_map/reduce_scatter | solution.py:30
  250.8 104.8 %reduce-scatter.8.cloned.1.call-done = f32[216,1280]{1,0:T(8,128)} async-done(((f32[1728,1280]{1,0:T(8,128)}), f32[216,1280]{1,0:T(8,128)}) %reduce-scatter.8.cloned.1.call-update) | async-done | bytes 1105936 | tf_op jit(solution)/shard_map/reduce_scatter | solution.py:31
  355.7 2.5 divide_convert_fusion
  358.2 0.0 all-gather.4.cloned.1.call-update
  358.2 0.0 reduce-scatter.10.cloned.1.call-start
  358.3 54.9 %all-gather.4.cloned.1.call-done = bf16[1728,1280]{1,0:T(8,128)(2,1)} async-done(((bf16[216,1280]{1,0:T(8,128)(2,1)}), bf16[1728,1280]{1,0:T(8,128)(2,1)}) %all-gather.4.cloned.1.call-update) | async-done | bytes 4423696 | tf_op jit(solution)/shard_map/all_gather | solution.py:34
  413.1 4.8 %fusion.7 = bf16[512,1280]{0,1:T(8,128)(2,1)S(1)} fusion(bf16[1728,1280]{1,0:T(8,128)(2,1)} %all-gather.4.cloned.1.call-done, bf16[1,512,1728]{1,2,0:T(8,128)(2,1)S(1)} %copy-done.1), kind=kOutput, calls=%fused_computation.9 | convolution fusion | flops 2265579520 | bytes 7503872 | tf_op jit(solution)/shard_map/dot_general | solution.py:36
  418.0 1.4 copy.8
  419.4 0.0 reduce-scatter.10.cloned.1.call-update
  419.4 42.9 %reduce-scatter.10.cloned.1.call-done = bf16[64,1280]{1,0:T(8,128)(2,1)} async-done(((bf16[512,1280]{1,0:T(8,128)(2,1)}), bf16[64,1280]{1,0:T(8,128)(2,1)}) %reduce-scatter.10.cloned.1.call-update) | async-done | bytes 163856
  462.4 1.1 copy.9
  463.5 0.8 copy.7
  464.3 4.6 copy.12
Async XLA Ops:
  7.2 136.4 %copy-start = (bf16[1,128,1280]{2,1,0:T(8,128)(2,1)S(1)}, bf16[1,128,1280]{2,1,0:T(8,128)(2,1)}, u32[]{:S(2)}) copy-start(bf16[1,128,1280]{2,1,0:T(8,128)(2,1)} %param.7) | copy-start | bytes 983044
  7.2 39.2 %all-gather.6.cloned.1.call-start = ((), (), s32[]{:S(2)}) async-start(), calls=%async_computation.7 | async-start | bytes 2211840 | tf_op jit(solution)/shard_map/all_gather | solution.py:20
  7.9 135.7 %copy-start.2 = (s32[1,512]{1,0:T(1,128)S(1)}, s32[1,512]{1,0:T(1,128)}, u32[]{:S(2)}) copy-start(s32[1,512]{1,0:T(1,128)} %param.6) | copy-start | bytes 6148
  7.9 135.7 %all-reduce.2.cloned.1.call-start = ((), (), s32[]{:S(2)}) async-start(), calls=%async_computation.3 | async-start | bytes 2621440 | tf_op jit(solution)/shard_map/psum | solution.py:22
  46.4 97.2 %copy-start.1 = (bf16[1,512,1728]{1,2,0:T(8,128)(2,1)S(1)}, bf16[1,512,1728]{1,2,0:T(8,128)(2,1)}, u32[]{:S(2)}) copy-start(bf16[1,512,1728]{1,2,0:T(8,128)(2,1)} %all-gather.6.cloned.1.call-done) | copy-start | bytes 5308420
  53.0 197.8 %reduce-scatter.6.cloned.1.call-start = ((), (), s32[]{:S(2)}) async-start(), calls=%async_computation.4 | async-start | bytes 9953280 | tf_op jit(solution)/shard_map/reduce_scatter | solution.py:30
  153.4 202.3 %reduce-scatter.8.cloned.1.call-start = ((), (), s32[]{:S(2)}) async-start(), calls=%async_computation.5 | async-start | bytes 9953280 | tf_op jit(solution)/shard_map/reduce_scatter | solution.py:31
  154.0 259.2 %all-gather.4.cloned.1.call-start = ((), (), s32[]{:S(2)}) async-start(), calls=%async_computation.6 | async-start | bytes 4976640 | tf_op jit(solution)/shard_map/all_gather | solution.py:34
  358.2 104.1 %reduce-scatter.10.cloned.1.call-start = ((), (), s32[]{:S(2)}) async-start(), calls=%async_computation.8 | async-start | bytes 1474560
Sparse Core Ops, SparseCore 0:
  9.8 36.5 all-gather.5
  53.1 90.4 all-reduce.1
  153.5 97.2 reduce-scatter.5
  253.4 102.1 reduce-scatter.7
  358.3 54.7 all-gather.3
  419.6 42.7 reduce-scatter.9
where the time goes:
time: 476 us
  waiting for transfers between devices  430 us (90%)
  matrix products  21.2 us (4%)
  between operations  14.1 us (3%)
  local copies, waits for them, and re-layouts  8.06 us (2%)
    reduce_scatter x1, waiting for transfers between devices, local(): lax.psum_scatter(fisher, 'task', scatter_dimension=0, tiled=True)  105 us
    reduce_scatter x1, waiting for transfers between devices, local(): lax.psum_scatter(weighted, 'task', scatter_dimension=0, tiled=True)  96.8 us
    psum x1, waiting for transfers between devices, local(): lax.psum(partial_out.astype(jnp.bfloat16), 'row').astype(jnp.float32)  90.5 us
    all_gather x1, waiting for transfers between devices, local(): merged = lax.all_gather(piece, 'task', axis=0, tiled=True)  54.9 us
    unnamed x7, waiting for transfers between devices  44.2 us
    all_gather x1, waiting for transfers between devices, local(): full_acts = lax.all_gather(acts, 'col', axis=0, tiled=True)  38.4 us
    dot_general x1, matrix products, local(): lax.dot_general(asq, gsq, (((0,), (0,)), ((), ())), preferred_element_typ...  9.77 us
  transfers between devices with their start and end apart: 6, of which 6 were waited for; matrix products, arithmetic and copies ran while one was open for 0% of the time, Pallas kernels for 0%

commit v1 on v0

--- a/solution.py
+++ b/solution.py
@@ -19,7 +19,9 @@
     protos = prototypes[0]
     full_acts = lax.all_gather(acts, "col", axis=0, tiled=True)
     partial_out = jnp.dot(full_acts, weight, preferred_element_type=jnp.float32)
-    output = lax.psum(partial_out.astype(jnp.bfloat16), "row").astype(jnp.float32)
+    output = jnp.sum(lax.all_gather(partial_out.astype(jnp.bfloat16), "row"), axis=0).astype(
+        jnp.float32
+    )
     grad = output - class_targets(label_row, protos)
     gsq = (grad * grad).astype(jnp.bfloat16)
     wide = full_acts.astype(jnp.float32)

time: 476 us -> 606 us (1.27)
  waiting for transfers between devices: 430 us -> 554 us
  other arithmetic: 2.53 us -> 8.89 us
    all_gather x0 -> x1, waiting for transfers between devices: none -> 212 us  [local(): lax.all_gather(partial_out.astype(jnp.bfloat16), 'row')]
    psum x1 -> x0, waiting for transfers between devices: 90.5 us -> none  [local(): lax.psum(partial_out.astype(jnp.bfloat16), 'row').astype(jnp.float32)]
    reduce_sum x0 -> x1, other arithmetic: none -> 6.36 us  [local(): jnp.sum(lax.all_gather(partial_out.astype(jnp.bfloat16), 'row'), axis=0)]
where the time goes in v1:
time: 606 us
  waiting for transfers between devices  554 us (91%)
  matrix products  20.7 us (3%)
  between operations  14.2 us (2%)
  other arithmetic  8.89 us (1%)
  local copies, waits for them, and re-layouts  8.05 us (1%)
    all_gather x1, waiting for transfers between devices, local(): lax.all_gather(partial_out.astype(jnp.bfloat16), 'row')  212 us
    reduce_scatter x1, waiting for transfers between devices, local(): lax.psum_scatter(fisher, 'task', scatter_dimension=0, tiled=True)  103 us
    reduce_scatter x1, waiting for transfers between devices, local(): lax.psum_scatter(weighted, 'task', scatter_dimension=0, tiled=True)  101 us
    all_gather x1, waiting for transfers between devices, local(): merged = lax.all_gather(piece, 'task', axis=0, tiled=True)  55.9 us
    unnamed x7, waiting for transfers between devices  44.2 us
    all_gather x1, waiting for transfers between devices, local(): full_acts = lax.all_gather(acts, 'col', axis=0, tiled=True)  38.4 us
  transfers between devices with their start and end apart: 6, of which 6 were waited for; matrix products, arithmetic and copies ran while one was open for 0% of the time, Pallas kernels for 0%

profile of v1, /device:TPU:8, one launch (start us, length us, event | category | flops | bytes accessed | tf_op | source)
XLA Modules:
  0.0 606.2 jit_solution(17296361397509422906)
XLA Ops:
  7.2 0.0 copy-start
  7.2 0.0 all-gather.8.cloned.1.call-start
  7.2 0.7 all-gather.8.cloned.1.call-update
  7.9 0.0 all-gather.10.cloned.1.call-start
  8.0 38.4 %all-gather.8.cloned.1.call-done = bf16[1,512,1728]{1,2,0:T(8,128)(2,1)} async-done(((bf16[1,128,1728]{1,2,0:T(8,128)(2,1)}), bf16[1,512,1728]{1,2,0:T(8,128)(2,1)}) %all-gather.8.cloned.1.call-update) | async-done | bytes 1769488 | tf_op jit(solution)/shard_map/all_gather | solution.py:20
  46.4 6.4 %fusion.4 = bf16[512,1280]{1,0:T(8,128)(2,1)} fusion(bf16[1,1728,1280]{2,1,0:T(8,128)(2,1)} %param.5, bf16[1,512,1728]{1,2,0:T(8,128)(2,1)} %all-gather.8.cloned.1.call-done), kind=kOutput, calls=%fused_computation.7 | convolution fusion | flops 2265579520 | bytes 7503872 | tf_op jit(solution)/shard_map/dot_general | solution.py:21
  52.9 0.0 all-gather.10.cloned.1.call-update
  52.9 0.0 reduce-scatter.6.cloned.1.call-start
  52.9 212.1 %all-gather.10.cloned.1.call-done = bf16[4096,1280]{1,0:T(8,128)(2,1)} async-done(((bf16[512,1280]{1,0:T(8,128)(2,1)}), bf16[4096,1280]{1,0:T(8,128)(2,1)}) %all-gather.10.cloned.1.call-update) | async-done | bytes 10485776 | tf_op jit(solution)/shard_map/all_gather | solution.py:22
  265.0 0.0 copy-start.1
  265.0 0.0 copy-start.2
  265.0 6.4 %reduce_sum.12 = bf16[512,1280]{1,0:T(8,128)(2,1)S(1)} reduce(bf16[8,512,1280]{2,1,0:T(8,128)(2,1)} %bitcast.30, bf16[]{:T(256)} %constant.1.clone.1), dimensions={0}, to_apply=%region_0.0 | reduce | flops 4587520 | bytes 11796482 | tf_op jit(solution)/shard_map/reduce_sum | solution.py:22
  271.4 0.0 copy-done
  271.4 0.0 copy-done.1
  271.4 0.0 copy-done.2
  271.4 9.4 %convert_multiply_fusion = (f32[1728,1280]{1,0:T(8,128)}, f32[1728,1280]{1,0:T(8,128)}) fusion(bf16[1,1728,1280]{2,1,0:T(8,128)(2,1)} %param.5, bf16[512,1280]{1,0:T(8,128)(2,1)S(1)} %reduce_sum.12, bf16[1,128,1280]{2,1,0:T(8,128)(2,1)S(1)} %copy-done, s32[512]{0:T(512)S(1)} %bitcast.32, bf16[1,512,1728]{1,2,0:T(8,128)(2,1)S(1)} %copy-done.1), kind=kOutput, calls=%fused_computation | convolution fusion | flops 2442461184 | bytes 25528320 | tf_op jit(solution)/shard_map/dot_general | solution.py:29
  280.8 0.0 reduce-scatter.6.cloned.1.call-update
  280.9 0.0 reduce-scatter.8.cloned.1.call-start
  280.9 0.5 reduce-scatter.8.cloned.1.call-update
  281.4 0.0 all-gather.6.cloned.1.call-start
  281.5 100.5 %reduce-scatter.6.cloned.1.call-done = f32[216,1280]{1,0:T(8,128)} async-done(((f32[1728,1280]{1,0:T(8,128)}), f32[216,1280]{1,0:T(8,128)}) %reduce-scatter.6.cloned.1.call-update) | async-done | bytes 1105936 | tf_op jit(solution)/shard_map/reduce_scatter | solution.py:32
  382.0 103.0 %reduce-scatter.8.cloned.1.call-done = f32[216,1280]{1,0:T(8,128)} async-done(((f32[1728,1280]{1,0:T(8,128)}), f32[216,1280]{1,0:T(8,128)}) %reduce-scatter.8.cloned.1.call-update) | async-done | bytes 1105936 | tf_op jit(solution)/shard_map/reduce_scatter | solution.py:33
  485.0 2.5 divide_convert_fusion
  487.5 0.0 all-gather.6.cloned.1.call-update
  487.6 0.0 reduce-scatter.10.cloned.1.call-start
  487.6 55.9 %all-gather.6.cloned.1.call-done = bf16[1728,1280]{1,0:T(8,128)(2,1)} async-done(((bf16[216,1280]{1,0:T(8,128)(2,1)}), bf16[1728,1280]{1,0:T(8,128)(2,1)}) %all-gather.6.cloned.1.call-update) | async-done | bytes 4423696 | tf_op jit(solution)/shard_map/all_gather | solution.py:36
  543.5 4.8 fusion.7
  548.4 1.4 copy.8
  549.8 0.0 reduce-scatter.10.cloned.1.call-update
  549.8 42.9 %reduce-scatter.10.cloned.1.call-done = bf16[64,1280]{1,0:T(8,128)(2,1)} async-done(((bf16[512,1280]{1,0:T(8,128)(2,1)}), bf16[64,1280]{1,0:T(8,128)(2,1)}) %reduce-scatter.10.cloned.1.call-update) | async-done | bytes 163856
  592.8 1.1 copy.9
  593.9 0.8 copy.7
  594.7 4.6 copy.11
Async XLA Ops:
  7.2 264.2 %copy-start = (bf16[1,128,1280]{2,1,0:T(8,128)(2,1)S(1)}, bf16[1,128,1280]{2,1,0:T(8,128)(2,1)}, u32[]{:S(2)}) copy-start(bf16[1,128,1280]{2,1,0:T(8,128)(2,1)} %param.7) | copy-start | bytes 983044
  7.2 39.2 %all-gather.8.cloned.1.call-start = ((), (), s32[]{:S(2)}) async-start(), calls=%async_computation.6 | async-start | bytes 2211840 | tf_op jit(solution)/shard_map/all_gather | solution.py:20
  7.9 257.1 %all-gather.10.cloned.1.call-start = ((), (), s32[]{:S(2)}) async-start(), calls=%async_computation.7 | async-start | bytes 11796480 | tf_op jit(solution)/shard_map/all_gather | solution.py:22
  52.9 329.1 %reduce-scatter.6.cloned.1.call-start = ((), (), s32[]{:S(2)}) async-start(), calls=%async_computation.3 | async-start | bytes 9953280 | tf_op jit(solution)/shard_map/reduce_scatter | solution.py:32
  265.0 6.4 %copy-start.1 = (bf16[1,512,1728]{1,2,0:T(8,128)(2,1)S(1)}, bf16[1,512,1728]{1,2,0:T(8,128)(2,1)}, u32[]{:S(2)}) copy-start(bf16[1,512,1728]{1,2,0:T(8,128)(2,1)} %all-gather.8.cloned.1.call-done) | copy-start | bytes 5308420
  265.0 6.4 %copy-start.2 = (s32[1,512]{1,0:T(1,128)S(1)}, s32[1,512]{1,0:T(1,128)}, u32[]{:S(2)}) copy-start(s32[1,512]{1,0:T(1,128)} %param.6) | copy-start | bytes 6148
  280.9 204.2 %reduce-scatter.8.cloned.1.call-start = ((), (), s32[]{:S(2)}) async-start(), calls=%async_computation.4 | async-start | bytes 9953280 | tf_op jit(solution)/shard_map/reduce_scatter | solution.py:33
  281.4 262.1 %all-gather.6.cloned.1.call-start = ((), (), s32[]{:S(2)}) async-start(), calls=%async_computation.5 | async-start | bytes 4976640 | tf_op jit(solution)/shard_map/all_gather | solution.py:36
  487.6 105.2 %reduce-scatter.10.cloned.1.call-start = ((), (), s32[]{:S(2)}) async-start(), calls=%async_computation.8 | async-start | bytes 1474560
Sparse Core Ops, SparseCore 0:
  9.8 36.5 all-gather.7
  53.0 211.9 all-gather.9
  281.0 100.9 reduce-scatter.5
  384.6 100.3 reduce-scatter.7
  487.7 55.7 all-gather.5
  550.0 42.7 reduce-scatter.9
